TPU v7x, 256 devices: a whole 4x4x8 slice. The times are simulated.
256 devices in a mesh: space: 32 (over x, z), col: 8 (over y, core).
Axes of the slice: x: 4, y: 4, z: 8, core: 2. Of those that a mesh axis runs over, the one named last changes fastest.
Arguments:
- blocks: bfloat16 [2560, 24, 128, 128], P('space', 'col'), may hold values from -0.109375 to 0.109375
- basis_tiles: bfloat16 [2560, 128, 128], P('space'), may hold values from -6 to 6
- weights: float32 [2560, 128], P('space'), may hold values from 0.1 to 1
- neighbour_device: int32 [2560, 24], P('space', 'col'), may hold values from 0 to 31, as said below
- neighbour_row: int32 [2560, 24], P('space', 'col'), may hold values from 0 to 79
- counts: int32 [2560], P('space'), may hold values from 12 to 24
- aggregate: int32 [2560], P('space'), may hold values from 0 to 9
- pair_slot: int32 [2560, 24], P('space', 'col'), may hold values from 0 to 3
Outputs:
- coarse: float32 [1280, 128, 128], P(('space', 'col'))
Inputs may be any that keep to these rules, and one draw needn't show every extreme that they name: `neighbour_device`: among the slots of one device's 80 rows that fall to one index of col, exactly 60 name another device; no other device is named more than 3 times there, and some other device exactly 3 times.
All inputs are finite; a program needn't handle non-finite values.
Results may differ from a plain program's by a relative error of at most 0.0045.
Values may be sent and summed in bfloat16 or wider, within the bound.
A program may use at most 128 MiB of HBM per device.

v0:
```python
import jax
import jax.numpy as jnp
from jax import lax
from jax.sharding import PartitionSpec as P

KC = 4
CAP = 3
NCD = 10


def per_device(
    blocks, basis_tiles, weights, neighbour_device, neighbour_row, counts, aggregate, pair_slot
):
    space_count = lax.axis_size("space")
    own_index = lax.axis_index("space")
    col_index = lax.axis_index("col")
    row_count, slot_count = neighbour_device.shape
    block_size = blocks.shape[2]
    coarse_size = basis_tiles.shape[2]
    slot_total = row_count * slot_count
    peer_of = neighbour_device.reshape(slot_total)
    row_of = neighbour_row.reshape(slot_total)
    remote = peer_of != own_index
    onehot = (
        (peer_of[:, None] == jnp.arange(space_count, dtype=jnp.int32)[None, :]) & remote[:, None]
    ).astype(jnp.int32)
    position = jnp.sum((jnp.cumsum(onehot, axis=0) - onehot) * onehot, axis=1)
    bucket = jnp.where(remote, peer_of * CAP + position, space_count * CAP)
    requests = jnp.zeros((space_count * CAP,), jnp.int32).at[bucket].set(row_of, mode="drop")
    requests = requests.reshape(space_count, CAP)
    asked_rows = lax.all_to_all(requests, "space", split_axis=0, concat_axis=0, tiled=True)
    tile_index = jnp.where(remote, row_count + bucket, row_of)
    received = lax.all_to_all(
        basis_tiles[asked_rows], "space", split_axis=0, concat_axis=0, tiled=True
    )
    tile_table = jnp.concatenate(
        [basis_tiles, received.reshape(space_count * CAP, block_size, coarse_size)], axis=0
    )
    fetched = tile_table[tile_index].reshape(row_count, slot_count, block_size, coarse_size)
    slot_number = col_index * slot_count + jnp.arange(slot_count, dtype=jnp.int32)
    usable = slot_number[None, :] < counts[:, None]
    masked = jnp.where(usable[:, :, None, None], blocks, jnp.zeros((), blocks.dtype))
    partial_sum = jnp.einsum("rkab,rkbc->rac", masked, fetched, preferred_element_type=jnp.float32)
    smoothed = lax.psum(partial_sum, "col")
    prolong = (basis_tiles.astype(jnp.float32) - weights[:, :, None] * smoothed).astype(
        jnp.bfloat16
    )
    received_prolong = lax.all_to_all(
        prolong[asked_rows], "space", split_axis=0, concat_axis=0, tiled=True
    )
    prolong_table = jnp.concatenate(
        [prolong, received_prolong.reshape(space_count * CAP, block_size, coarse_size)], axis=0
    )
    neighbour_prolong = prolong_table[tile_index].reshape(
        row_count, slot_count, block_size, coarse_size
    )
    applied = jnp.einsum(
        "rkab,rkbc->rkac", masked, neighbour_prolong, preferred_element_type=jnp.float32
    ).astype(jnp.bfloat16)
    contribution = jnp.einsum(
        "rad,rkae->rkde", prolong, applied, preferred_element_type=jnp.float32
    )
    targets = (aggregate[:, None] * KC + pair_slot).reshape(slot_total)
    coarse_local = jax.ops.segment_sum(
        contribution.reshape(slot_total, coarse_size, coarse_size), targets, num_segments=NCD * KC
    )
    return lax.psum_scatter(coarse_local, "col", scatter_dimension=0, tiled=True)


def solution(mesh):
    return jax.shard_map(
        per_device,
        mesh=mesh,
        in_specs=(
            P("space", "col", None, None),
            P("space", None, None),
            P("space", None),
            P("space", "col"),
            P("space", "col"),
            P("space"),
            P("space"),
            P("space", "col"),
        ),
        out_specs=P(("space", "col"), None, None),
        check_vma=False,
    )
```

profile of v0, /device:TPU:6, one launch (start us, length us, event | category | flops | bytes accessed | tf_op | source)
XLA Modules:
  0.0 429.7 jit_solution(17318623963266410459)
XLA Ops:
  6.5 0.8 copy.26
  7.3 0.7 broadcast_multiply_fusion
  8.0 0.8 copy.29
  8.9 0.2 reshape.224
  9.1 0.2 eq.22
  9.2 0.7 broadcast_compare_fusion.1
  10.0 0.6 reduce-window.6
  10.6 0.2 slice_reduce_fusion
  11.0 0.2 ne.29
  11.3 0.2 mul.47
  11.5 1.3 scatter_custom_fusion
  12.9 19.3 %all_to_all.22 = s32[32,1,3]{2,1,0:T(1,128)S(1)} all-to-all(s32[32,1,3]{2,1,0:T(1,128)S(1)} %bitcast.44), channel_id=1, replica_groups=mesh['space'=32,'col'=8] {'space'}, dimensions={0} | all-to-all | bytes 768 | tf_op jit(solution)/shard_map/all_to_all | solution.py:31
  32.6 4.6 %gather_fusion = bf16[96,128,128]{2,1,0:T(8,128)(2,1)} fusion(bf16[80,128,128]{2,1,0:T(8,128)(2,1)} %param.9, s32[1024]{0:T(1024)S(1)} %pad_clamp_fusion.1), kind=kCustom, calls=%fused_computation | custom fusion | bytes 6291840 | tf_op jit(solution)/shard_map/gather | solution.py:34
  37.2 6.6 %all-to-all-start.1 = ((bf16[32,3,128,128]{3,2,1,0:T(8,128)(2,1)}), bf16[32,3,128,128]{3,2,1,0:T(8,128)(2,1)}, u32[]{:S(2)}, u32[]{:S(2)}) async-start(bf16[32,3,128,128]{3,2,1,0:T(8,128)(2,1)} %bitcast.41), calls=%async_computation.1 | async-start | bytes 6291456 | tf_op jit(solution)/shard_map/all_to_all | solution.py:33
  44.0 71.3 %all-to-all-done.1 = bf16[32,3,128,128]{3,2,1,0:T(8,128)(2,1)} async-done(((bf16[32,3,128,128]{3,2,1,0:T(8,128)(2,1)}), bf16[32,3,128,128]{3,2,1,0:T(8,128)(2,1)}, u32[]{:S(2)}, u32[]{:S(2)}) %all-to-all-start.1) | async-done | bytes 3145760 | tf_op jit(solution)/shard_map/all_to_all | solution.py:33
  115.3 4.9 %pad_maximum_fusion = bf16[176,128,128]{2,1,0:T(8,128)(2,1)} fusion(bf16[96,128,128]{2,1,0:T(8,128)(2,1)} %bitcast.6, bf16[80,128,128]{2,1,0:T(8,128)(2,1)S(1)} %copy-done.1), kind=kLoop, calls=%fused_computation.11 | loop fusion | flops 2883584 | bytes 11534336 | tf_op jit(solution)/shard_map/concatenate | solution.py:36
  120.2 11.1 %gather_fusion.1 = bf16[240,128,128]{2,1,0:T(8,128)(2,1)} fusion(bf16[176,128,128]{2,1,0:T(8,128)(2,1)} %pad_maximum_fusion, s32[1024]{0:T(1024)S(1)} %pad_clamp_fusion), kind=kCustom, calls=%fused_computation.1 | custom fusion | bytes 15729600 | tf_op jit(solution)/shard_map/gather | solution.py:39
  131.4 10.1 %fusion.8 = f32[80,128,128]{2,1,0:T(8,128)} fusion(bf16[80,3,128,128]{3,2,1,0:T(8,128)(2,1)} %bitcast.43, bf16[80,3,128,128]{3,2,1,0:T(8,128)(2,1)} %param.8, pred[80,3]{1,0:T(8,128)(4,1)S(1)} %broadcast_compare_fusion), kind=kOutput, calls=%fused_computation.17 | convolution fusion | flops 1010565120 | bytes 20971760 | tf_op jit(solution)/shard_map/rkab,rkbc->rac/dot_general | solution.py:43
  141.4 79.2 %all-reduce.3.cloned.1.call-done = f32[80,128,128]{2,1,0:T(8,128)} async-done(((f32[80,128,128]{2,1,0:T(8,128)}), f32[80,128,128]{2,1,0:T(8,128)}) %all-reduce.3.cloned.1.call-update) | async-done | bytes 5242896 | tf_op jit(solution)/shard_map/psum | solution.py:44
  220.7 4.6 %subtract_convert_fusion = bf16[80,128,128]{2,1,0:T(8,128)(2,1)S(1)} fusion(f32[80,128,128]{2,1,0:T(8,128)} %all-reduce.3.cloned.1.call-done, bf16[80,128,128]{2,1,0:T(8,128)(2,1)} %param.9, f32[80,128]{1,0:T(8,128)S(1)} %copy-done.2), kind=kLoop, calls=%fused_computation.13 | loop fusion | flops 5242880 | bytes 10526720 | tf_op jit(solution)/shard_map/convert_element_type | solution.py:45
  225.3 2.7 gather_fusion.2
  228.0 10.2 %all-to-all-start.2 = ((bf16[32,3,128,128]{3,2,1,0:T(8,128)(2,1)}), bf16[32,3,128,128]{3,2,1,0:T(8,128)(2,1)}, u32[]{:S(2)}, u32[]{:S(2)}) async-start(bf16[32,3,128,128]{3,2,1,0:T(8,128)(2,1)} %bitcast.42), calls=%async_computation.2 | async-start | bytes 6291456 | tf_op jit(solution)/shard_map/all_to_all | solution.py:48
  238.3 0.2 reduce-scatter.2.cloned.1.call-start
  238.8 71.7 %all-to-all-done.2 = bf16[32,3,128,128]{3,2,1,0:T(8,128)(2,1)} async-done(((bf16[32,3,128,128]{3,2,1,0:T(8,128)(2,1)}), bf16[32,3,128,128]{3,2,1,0:T(8,128)(2,1)}, u32[]{:S(2)}, u32[]{:S(2)}) %all-to-all-start.2) | async-done | bytes 3145760 | tf_op jit(solution)/shard_map/all_to_all | solution.py:48
  310.5 4.9 %pad_maximum_fusion.1 = bf16[176,128,128]{2,1,0:T(8,128)(2,1)} fusion(bf16[96,128,128]{2,1,0:T(8,128)(2,1)} %bitcast.12, bf16[80,128,128]{2,1,0:T(8,128)(2,1)S(1)} %subtract_convert_fusion), kind=kLoop, calls=%fused_computation.12 | loop fusion | flops 2883584 | bytes 11534336 | tf_op jit(solution)/shard_map/concatenate | solution.py:51
  315.4 11.1 %gather_fusion.3 = bf16[240,128,128]{2,1,0:T(8,128)(2,1)} fusion(bf16[176,128,128]{2,1,0:T(8,128)(2,1)} %pad_maximum_fusion.1, s32[1024]{0:T(1024)S(1)} %pad_clamp_fusion), kind=kCustom, calls=%fused_computation.3 | custom fusion | bytes 15729600 | tf_op jit(solution)/shard_map/gather | solution.py:54
  326.5 11.1 %fusion = f32[80,3,128,128]{3,2,1,0:T(8,128)} fusion(bf16[80,3,128,128]{3,2,1,0:T(8,128)(2,1)} %bitcast.40, bf16[80,3,128,128]{3,2,1,0:T(8,128)(2,1)} %param.8, pred[80,3]{1,0:T(8,128)(4,1)S(1)} %broadcast_compare_fusion, bf16[80,128,128]{2,1,0:T(8,128)(2,1)S(1)} %subtract_convert_fusion), kind=kOutput, calls=%fused_computation.6 | convolution fusion | flops 2021130240 | bytes 34078960 | tf_op jit(solution)/shard_map/rad,rkae->rkde/dot_general | solution.py:60
  337.6 15.7 %copy.35 = f32[240,128,128]{2,1,0:T(8,128)} copy(f32[240,128,128]{1,2,0:T(8,128)} %bitcast.39) | data formatting | bytes 31457280 | tf_op jit(solution)/shard_map/reshape | solution.py:65
  353.3 0.3 broadcast_in_dim.20
  353.6 31.5 %scatter_fusion = f32[40,128,128]{2,1,0:T(8,128)S(1)} fusion(f32[40,128,128]{2,1,0:T(8,128)S(1)} %broadcast_in_dim.20, s32[240]{0:T(256)S(1)} %reshape.230, f32[240,128,128]{2,1,0:T(8,128)} %copy.35), kind=kCustom, calls=%fused_computation.5 | custom fusion | flops 3932160 | bytes 47186880 | tf_op jit(solution)/shard_map/scatter-add | solution.py:64
  385.1 1.5 copy-done
  386.7 36.2 %reduce-scatter.2.cloned.1.call-done = f32[5,128,128]{2,1,0:T(8,128)} async-done(((f32[40,128,128]{2,1,0:T(8,128)}), f32[5,128,128]{2,1,0:T(8,128)}) %reduce-scatter.2.cloned.1.call-update) | async-done | bytes 327696 | tf_op jit(solution)/shard_map/reduce_scatter | solution.py:67
  (38 shorter events, 1.4 us)
Async XLA Ops:
  32.6 11.4 %copy-start.4 = (s32[80]{0:T(128)S(1)}, s32[80]{0:T(128)}, u32[]{:S(2)}) copy-start(s32[80]{0:T(128)} %param.13) | copy-start | bytes 964
  32.6 82.7 %copy-start.1 = (bf16[80,128,128]{2,1,0:T(8,128)(2,1)S(1)}, bf16[80,128,128]{2,1,0:T(8,128)(2,1)}, u32[]{:S(2)}) copy-start(bf16[80,128,128]{2,1,0:T(8,128)(2,1)} %param.9) | copy-start | bytes 7864324
  37.2 78.1 %all-to-all-start.1 = ((bf16[32,3,128,128]{3,2,1,0:T(8,128)(2,1)}), bf16[32,3,128,128]{3,2,1,0:T(8,128)(2,1)}, u32[]{:S(2)}, u32[]{:S(2)}) async-start(bf16[32,3,128,128]{3,2,1,0:T(8,128)(2,1)} %bitcast.41), calls=%async_computation.1 | async-start | bytes 6291456 | tf_op jit(solution)/shard_map/all_to_all | solution.py:33
  43.9 176.8 %all-reduce.3.cloned.1.call-start = ((), (), s32[]{:S(2)}) async-start(), calls=%async_computation.4 | async-start | bytes 10485760 | tf_op jit(solution)/shard_map/psum | solution.py:44
  131.4 89.3 %copy-start.2 = (f32[80,128]{1,0:T(8,128)S(1)}, f32[80,128]{1,0:T(8,128)}, u32[]{:S(2)}) copy-start(f32[80,128]{1,0:T(8,128)} %param.10) | copy-start | bytes 122884
  225.3 13.2 %copy-start.5 = (s32[80]{0:T(128)S(1)}, s32[80]{0:T(128)}, u32[]{:S(2)}) copy-start(s32[80]{0:T(128)} %param.14) | copy-start | bytes 964
  225.3 13.2 %copy-start.3 = (s32[80,3]{0,1:T(4,128)S(1)}, s32[80,3]{0,1:T(4,128)}, u32[]{:S(2)}) copy-start(s32[80,3]{0,1:T(4,128)} %param.15) | copy-start | bytes 2884
  228.0 82.5 %all-to-all-start.2 = ((bf16[32,3,128,128]{3,2,1,0:T(8,128)(2,1)}), bf16[32,3,128,128]{3,2,1,0:T(8,128)(2,1)}, u32[]{:S(2)}, u32[]{:S(2)}) async-start(bf16[32,3,128,128]{3,2,1,0:T(8,128)(2,1)} %bitcast.42), calls=%async_computation.2 | async-start | bytes 6291456 | tf_op jit(solution)/shard_map/all_to_all | solution.py:48
  238.3 184.5 %reduce-scatter.2.cloned.1.call-start = ((), (), s32[]{:S(2)}) async-start(), calls=%async_computation.5 | async-start | bytes 2949120 | tf_op jit(solution)/shard_map/reduce_scatter | solution.py:67
  385.1 1.5 copy-start
Sparse Core Ops, SparseCore 0:
  141.6 79.0 all-reduce.2
  386.8 35.9 reduce-scatter.1
where the time goes:
time: 431 us; the launch traced here: 430 us
  waiting for transfers between devices  258 us (60%)
  local copies, waits for them, and re-layouts  51.8 us (12%)
  other arithmetic  48.2 us (11%)
  matrix products  21.2 us (5%)
  blocking collectives  19.3 us (4%)
  starting transfers between devices  17.1 us (4%)
  between operations  13.6 us (3%)
    psum x1, waiting for transfers between devices, per_device(): smoothed = lax.psum(partial_sum, 'col')  79.2 us
    all_to_all x1, waiting for transfers between devices, per_device(): lax.all_to_all(prolong[asked_rows], 'space', split_axis=0, concat_axis=0,...  71.7 us
    all_to_all x1, waiting for transfers between devices, per_device(): lax.all_to_all(basis_tiles[asked_rows], 'space', split_axis=0, concat_axi...  71.3 us
    reduce_scatter x1, waiting for transfers between devices, per_device(): lax.psum_scatter(coarse_local, 'col', scatter_dimension=0, tiled=True)  36.2 us
    scatter-add x1, other arithmetic, per_device(): jax.ops.segment_sum(contribution.reshape(slot_total, coarse_size, coarse_...  31.5 us
    all_to_all x1, blocking collectives, per_device(): lax.all_to_all(requests, 'space', split_axis=0, concat_axis=0, tiled=True)  19.3 us
    reshape x1, local copies, waits for them, and re-layouts, per_device(): contribution.reshape(slot_total, coarse_size, coarse_size)  15.7 us
    gather x1, local copies, waits for them, and re-layouts, per_device(): prolong_table[tile_index]  11.1 us
  transfers between devices with their start and end apart: 4, of which 4 were waited for; matrix products, arithmetic and copies ran while one was open for 0% of the time, Pallas kernels for 0%

commit v1 on v0

--- a/solution.py
+++ b/solution.py
@@ -6,6 +6,14 @@
 KC = 4
 CAP = 3
 NCD = 10
+
+
+def add_in_pairs(value, axis):
+    count, summed = (lax.axis_size(axis), value)
+    for far in [1 << k for k in range(count.bit_length() - 1)]:
+        pairs = [(i, i ^ far) for i in range(count)]
+        summed = summed + lax.ppermute(summed, axis, pairs)
+    return summed
 
 
 def per_device(
@@ -41,7 +49,7 @@
     usable = slot_number[None, :] < counts[:, None]
     masked = jnp.where(usable[:, :, None, None], blocks, jnp.zeros((), blocks.dtype))
     partial_sum = jnp.einsum("rkab,rkbc->rac", masked, fetched, preferred_element_type=jnp.float32)
-    smoothed = lax.psum(partial_sum, "col")
+    smoothed = add_in_pairs(partial_sum, "col")
     prolong = (basis_tiles.astype(jnp.float32) - weights[:, :, None] * smoothed).astype(
         jnp.bfloat16
     )

time: 431 us -> 584 us (1.35)
  waiting for transfers between devices: 258 us -> 412 us
    ppermute x0 -> x3, waiting for transfers between devices: none -> 235 us  [add_in_pairs(): summed = summed + lax.ppermute(summed, axis, pairs)]
    psum x1 -> x0, waiting for transfers between devices: 79.2 us -> none  [per_device(): smoothed = lax.psum(partial_sum, 'col')]
  transfers between devices with their start and end apart: 4 -> 6, of which waited for: 4 -> 6; matrix products, arithmetic and copies ran while one was open for 0% -> 0% of each run, Pallas kernels for 0% -> 0%
where the time goes in v1:
time: 584 us; the launch traced here: 583 us
  waiting for transfers between devices  412 us (71%)
  local copies, waits for them, and re-layouts  51.8 us (9%)
  other arithmetic  48.4 us (8%)
  blocking collectives  19.3 us (3%)
  matrix products  18.8 us (3%)
  starting transfers between devices  18.7 us (3%)
  between operations  13.7 us (2%)
    ppermute x3, waiting for transfers between devices, add_in_pairs(): summed = summed + lax.ppermute(summed, axis, pairs)  235 us
    all_to_all x1, waiting for transfers between devices, per_device(): lax.all_to_all(basis_tiles[asked_rows], 'space', split_axis=0, concat_axi...  71.3 us
    all_to_all x1, waiting for transfers between devices, per_device(): lax.all_to_all(prolong[asked_rows], 'space', split_axis=0, concat_axis=0,...  71.1 us
    reduce_scatter x1, waiting for transfers between devices, per_device(): lax.psum_scatter(coarse_local, 'col', scatter_dimension=0, tiled=True)  35.2 us
    scatter-add x1, other arithmetic, per_device(): jax.ops.segment_sum(contribution.reshape(slot_total, coarse_size, coarse_...  31.5 us
    all_to_all x1, blocking collectives, per_device(): lax.all_to_all(requests, 'space', split_axis=0, concat_axis=0, tiled=True)  19.3 us
    reshape x1, local copies, waits for them, and re-layouts, per_device(): contribution.reshape(slot_total, coarse_size, coarse_size)  15.7 us
  transfers between devices with their start and end apart: 6, of which 6 were waited for; matrix products, arithmetic and copies ran while one was open for 0% of the time, Pallas kernels for 0%

profile of v1, /device:TPU:6, one launch (start us, length us, event | category | flops | bytes accessed | tf_op | source)
XLA Modules:
  0.0 583.1 jit_solution(3059425702327754791)
XLA Ops:
  6.5 0.8 copy.26
  7.3 0.7 broadcast_multiply_fusion
  8.0 0.8 copy.29
  9.2 0.7 broadcast_compare_fusion.1
  10.0 0.6 reduce-window.6
  11.5 1.3 scatter_custom_fusion
  12.9 19.3 %all_to_all.22 = s32[32,1,3]{2,1,0:T(1,128)S(1)} all-to-all(s32[32,1,3]{2,1,0:T(1,128)S(1)} %bitcast.44), channel_id=1, replica_groups=mesh['space'=32,'col'=8] {'space'}, dimensions={0} | all-to-all | bytes 768 | tf_op jit(solution)/shard_map/all_to_all | solution.py:39
  32.6 4.6 gather_fusion
  37.2 6.6 %all-to-all-start.1 = ((bf16[32,3,128,128]{3,2,1,0:T(8,128)(2,1)}), bf16[32,3,128,128]{3,2,1,0:T(8,128)(2,1)}, u32[]{:S(2)}, u32[]{:S(2)}) async-start(bf16[32,3,128,128]{3,2,1,0:T(8,128)(2,1)} %bitcast.41), calls=%async_computation.1 | async-start | bytes 6291456 | tf_op jit(solution)/shard_map/all_to_all | solution.py:41
  44.0 71.3 %all-to-all-done.1 = bf16[32,3,128,128]{3,2,1,0:T(8,128)(2,1)} async-done(((bf16[32,3,128,128]{3,2,1,0:T(8,128)(2,1)}), bf16[32,3,128,128]{3,2,1,0:T(8,128)(2,1)}, u32[]{:S(2)}, u32[]{:S(2)}) %all-to-all-start.1) | async-done | bytes 3145760 | tf_op jit(solution)/shard_map/all_to_all | solution.py:41
  115.3 4.9 pad_maximum_fusion
  120.2 11.1 %gather_fusion.1 = bf16[240,128,128]{2,1,0:T(8,128)(2,1)} fusion(bf16[176,128,128]{2,1,0:T(8,128)(2,1)} %pad_maximum_fusion, s32[1024]{0:T(1024)S(1)} %pad_clamp_fusion), kind=kCustom, calls=%fused_computation.1 | custom fusion | bytes 15729600 | tf_op jit(solution)/shard_map/gather | solution.py:47
  131.4 7.7 %fusion.8 = f32[80,128,128]{2,1,0:T(8,128)S(1)} fusion(bf16[80,3,128,128]{3,2,1,0:T(8,128)(2,1)} %bitcast.43, bf16[80,3,128,128]{3,2,1,0:T(8,128)(2,1)} %param.8, pred[80,3]{1,0:T(8,128)(4,1)S(1)} %broadcast_compare_fusion), kind=kOutput, calls=%fused_computation.17 | convolution fusion | flops 1010565120 | bytes 20971760 | tf_op jit(solution)/shard_map/rkab,rkbc->rac/dot_general | solution.py:51
  139.2 8.6 %collective-permute-done = f32[80,128,128]{2,1,0:T(8,128)S(1)} collective-permute-done((f32[80,128,128]{2,1,0:T(8,128)S(1)}, f32[80,128,128]{2,1,0:T(8,128)S(1)}, u32[]{:S(2)}, u32[]{:S(2)}) %collective-permute-start) | collective-permute-done | bytes 5242912 | tf_op jit(solution)/shard_map/ppermute | solution.py:15
  147.9 1.5 add.101
  149.4 1.8 collective-permute-start.1
  151.2 113.5 %collective-permute-done.1 = f32[80,128,128]{2,1,0:T(8,128)S(1)} collective-permute-done((f32[80,128,128]{2,1,0:T(8,128)S(1)}, f32[80,128,128]{2,1,0:T(8,128)S(1)}, u32[]{:S(2)}, u32[]{:S(2)}) %collective-permute-start.1) | collective-permute-done | bytes 5242912 | tf_op jit(solution)/shard_map/ppermute | solution.py:15
  264.7 1.5 add.102
  266.2 3.3 collective-permute-start.2
  269.5 112.5 %collective-permute-done.2 = f32[80,128,128]{2,1,0:T(8,128)S(1)} collective-permute-done((f32[80,128,128]{2,1,0:T(8,128)S(1)}, f32[80,128,128]{2,1,0:T(8,128)S(1)}, u32[]{:S(2)}, u32[]{:S(2)}) %collective-permute-start.2) | collective-permute-done | bytes 5242912 | tf_op jit(solution)/shard_map/ppermute | solution.py:15
  382.0 1.9 subtract_convert_fusion
  383.9 2.7 gather_fusion.2
  386.6 6.8 %all-to-all-start.2 = ((bf16[32,3,128,128]{3,2,1,0:T(8,128)(2,1)}), bf16[32,3,128,128]{3,2,1,0:T(8,128)(2,1)}, u32[]{:S(2)}, u32[]{:S(2)}) async-start(bf16[32,3,128,128]{3,2,1,0:T(8,128)(2,1)} %bitcast.42), calls=%async_computation.2 | async-start | bytes 6291456 | tf_op jit(solution)/shard_map/all_to_all | solution.py:56
  393.8 71.1 %all-to-all-done.2 = bf16[32,3,128,128]{3,2,1,0:T(8,128)(2,1)} async-done(((bf16[32,3,128,128]{3,2,1,0:T(8,128)(2,1)}), bf16[32,3,128,128]{3,2,1,0:T(8,128)(2,1)}, u32[]{:S(2)}, u32[]{:S(2)}) %all-to-all-start.2) | async-done | bytes 3145760 | tf_op jit(solution)/shard_map/all_to_all | solution.py:56
  464.9 4.9 pad_maximum_fusion.1
  469.8 11.1 %gather_fusion.3 = bf16[240,128,128]{2,1,0:T(8,128)(2,1)} fusion(bf16[176,128,128]{2,1,0:T(8,128)(2,1)} %pad_maximum_fusion.1, s32[1024]{0:T(1024)S(1)} %pad_clamp_fusion), kind=kCustom, calls=%fused_computation.3 | custom fusion | bytes 15729600 | tf_op jit(solution)/shard_map/gather | solution.py:62
  480.9 11.1 %fusion = f32[80,3,128,128]{3,2,1,0:T(8,128)} fusion(bf16[80,3,128,128]{3,2,1,0:T(8,128)(2,1)} %bitcast.40, bf16[80,3,128,128]{3,2,1,0:T(8,128)(2,1)} %param.8, pred[80,3]{1,0:T(8,128)(4,1)S(1)} %broadcast_compare_fusion, bf16[80,128,128]{2,1,0:T(8,128)(2,1)S(1)} %subtract_convert_fusion), kind=kOutput, calls=%fused_computation.6 | convolution fusion | flops 2021130240 | bytes 34078960 | tf_op jit(solution)/shard_map/rad,rkae->rkde/dot_general | solution.py:68
  492.0 15.7 %copy.35 = f32[240,128,128]{2,1,0:T(8,128)} copy(f32[240,128,128]{1,2,0:T(8,128)} %bitcast.39) | data formatting | bytes 31457280 | tf_op jit(solution)/shard_map/reshape | solution.py:73
  507.7 0.3 broadcast_in_dim.20
  508.0 31.5 %scatter_fusion = f32[40,128,128]{2,1,0:T(8,128)S(1)} fusion(f32[40,128,128]{2,1,0:T(8,128)S(1)} %broadcast_in_dim.20, s32[240]{0:T(256)S(1)} %reshape.230, f32[240,128,128]{2,1,0:T(8,128)} %copy.35), kind=kCustom, calls=%fused_computation.5 | custom fusion | flops 3932160 | bytes 47186880 | tf_op jit(solution)/shard_map/scatter-add | solution.py:72
  539.5 1.5 copy-done
  541.1 35.2 %reduce-scatter.2.cloned.1.call-done = f32[5,128,128]{2,1,0:T(8,128)} async-done(((f32[40,128,128]{2,1,0:T(8,128)}), f32[5,128,128]{2,1,0:T(8,128)}) %reduce-scatter.2.cloned.1.call-update) | async-done | bytes 327696 | tf_op jit(solution)/shard_map/reduce_scatter | solution.py:75
  (45 shorter events, 2.3 us)
Async XLA Ops:
  32.6 11.3 %copy-start.5 = (s32[80]{0:T(128)S(1)}, s32[80]{0:T(128)}, u32[]{:S(2)}) copy-start(s32[80]{0:T(128)} %param.13) | copy-start | bytes 964
  32.6 82.7 %copy-start.1 = (bf16[80,128,128]{2,1,0:T(8,128)(2,1)S(1)}, bf16[80,128,128]{2,1,0:T(8,128)(2,1)}, u32[]{:S(2)}) copy-start(bf16[80,128,128]{2,1,0:T(8,128)(2,1)} %param.9) | copy-start | bytes 7864324
  37.2 78.1 %all-to-all-start.1 = ((bf16[32,3,128,128]{3,2,1,0:T(8,128)(2,1)}), bf16[32,3,128,128]{3,2,1,0:T(8,128)(2,1)}, u32[]{:S(2)}, u32[]{:S(2)}) async-start(bf16[32,3,128,128]{3,2,1,0:T(8,128)(2,1)} %bitcast.41), calls=%async_computation.1 | async-start | bytes 6291456 | tf_op jit(solution)/shard_map/all_to_all | solution.py:41
  139.1 8.7 %collective-permute-start = (f32[80,128,128]{2,1,0:T(8,128)S(1)}, f32[80,128,128]{2,1,0:T(8,128)S(1)}, u32[]{:S(2)}, u32[]{:S(2)}) collective-permute-start(f32[80,128,128]{2,1,0:T(8,128)S(1)} %fusion.8), channel_id=1, source_target_pairs={{0,1},{1,0},{2,3},{3,2},{4,5},{5,4},{6,7},{7,6},{8,9},{9,8},{10,11... | collective-permute-start | bytes 15728648 | tf_op jit(solution)/shard_map/ppermute | solution.py:15
  149.3 232.7 %copy-start.2 = (bf16[80,128,128]{2,1,0:T(8,128)(2,1)S(1)}, bf16[80,128,128]{2,1,0:T(8,128)(2,1)}, u32[]{:S(2)}) copy-start(bf16[80,128,128]{2,1,0:T(8,128)(2,1)} %param.9) | copy-start | bytes 7864324
  149.4 232.7 %copy-start.3 = (f32[80,128]{1,0:T(8,128)S(1)}, f32[80,128]{1,0:T(8,128)}, u32[]{:S(2)}) copy-start(f32[80,128]{1,0:T(8,128)} %param.10) | copy-start | bytes 122884
  149.4 115.4 %collective-permute-start.1 = (f32[80,128,128]{2,1,0:T(8,128)S(1)}, f32[80,128,128]{2,1,0:T(8,128)S(1)}, u32[]{:S(2)}, u32[]{:S(2)}) collective-permute-start(f32[80,128,128]{2,1,0:T(8,128)S(1)} %add.101), channel_id=1, source_target_pairs={{0,2},{1,3},{2,0},{3,1},{4,6},{5,7},{6,4},{7,5},{8,10},{9,11},{10,... | collective-permute-start | bytes 15728648 | tf_op jit(solution)/shard_map/ppermute | solution.py:15
  266.2 115.8 %collective-permute-start.2 = (f32[80,128,128]{2,1,0:T(8,128)S(1)}, f32[80,128,128]{2,1,0:T(8,128)S(1)}, u32[]{:S(2)}, u32[]{:S(2)}) collective-permute-start(f32[80,128,128]{2,1,0:T(8,128)S(1)} %add.102), channel_id=1, source_target_pairs={{0,4},{1,5},{2,6},{3,7},{4,0},{5,1},{6,2},{7,3},{8,12},{9,13},{10,... | collective-permute-start | bytes 15728648 | tf_op jit(solution)/shard_map/ppermute | solution.py:15
  383.9 9.6 %copy-start.6 = (s32[80]{0:T(128)S(1)}, s32[80]{0:T(128)}, u32[]{:S(2)}) copy-start(s32[80]{0:T(128)} %param.14) | copy-start | bytes 964
  383.9 9.6 %copy-start.4 = (s32[80,3]{0,1:T(4,128)S(1)}, s32[80,3]{0,1:T(4,128)}, u32[]{:S(2)}) copy-start(s32[80,3]{0,1:T(4,128)} %param.15) | copy-start | bytes 2884
  386.6 78.3 %all-to-all-start.2 = ((bf16[32,3,128,128]{3,2,1,0:T(8,128)(2,1)}), bf16[32,3,128,128]{3,2,1,0:T(8,128)(2,1)}, u32[]{:S(2)}, u32[]{:S(2)}) async-start(bf16[32,3,128,128]{3,2,1,0:T(8,128)(2,1)} %bitcast.42), calls=%async_computation.2 | async-start | bytes 6291456 | tf_op jit(solution)/shard_map/all_to_all | solution.py:56
  393.5 182.7 %reduce-scatter.2.cloned.1.call-start = ((), (), s32[]{:S(2)}) async-start(), calls=%async_computation.4 | async-start | bytes 2949120 | tf_op jit(solution)/shard_map/reduce_scatter | solution.py:75
  539.5 1.5 copy-start
Sparse Core Ops, SparseCore 0:
  541.2 34.9 reduce-scatter.1
